TPU v7x, 512 devices: a whole 4x8x8 slice. The times are simulated.
512 devices in a mesh: tok: 64 (over z, y), tp: 8 (over x, core).
Axes of the slice: x: 4, y: 8, z: 8, core: 2. Of those that a mesh axis runs over, the one named last changes fastest.
Arguments:
- activations: bfloat16 [8192, 4096], P('tok', 'tp'), may hold values from -6 to 6
- out_grad: bfloat16 [8192, 4096], P('tok', 'tp'), may hold values from -6 to 6
- routes: int32 [8192, 2], P('tok'), may hold values from 0 to 63, all different within a row; in each aligned block of 128 rows (0 to 127, 128 to 255, ...) at most 8 rows name the same one
- gate_vals: float32 [8192, 2], P('tok'), may hold values from 0.2 to 1
- w_gate: bfloat16 [64, 1536, 4096], P('tok', 'tp'), may hold values from -0.09375 to 0.09375
- w_up: bfloat16 [64, 1536, 4096], P('tok', 'tp'), may hold values from -0.09375 to 0.09375
- w_down: bfloat16 [64, 1536, 4096], P('tok', 'tp'), may hold values from -0.15625 to 0.15625
Outputs:
- in_grad: bfloat16 [8192, 4096], P('tok', 'tp')
Inputs may be any that keep to these rules, and one draw needn't show every extreme that they name: `routes`: each row names 2 different experts. In each aligned block of 128 rows (the tokens of one index of tok) no expert is named by more than 8 rows, a bound that some block reaches.
All inputs are finite; a program needn't handle non-finite values.
Results may differ from a plain program's by a relative error of at most 0.0057.
Values may be sent and summed in bfloat16 or wider, within the bound.
No kernel may reach another device: no remote copies, remote signals or barrier semaphores. Data moves between devices by JAX's collectives and lax.ppermute only.
A program may use at most 64 MiB of HBM per device.

v0:
```python
import jax
import jax.numpy as jnp
from jax import lax
from jax.sharding import PartitionSpec as P


def routing(routes, n_tok, capacity):
    tok_dev = routes.shape[0]
    top_k = routes.shape[1]
    flat = routes.reshape(-1)
    onehot = (flat[:, None] == jnp.arange(n_tok, dtype=jnp.int32)[None, :]).astype(jnp.int32)
    before = jnp.cumsum(onehot, axis=0) - onehot
    slot = jnp.sum(before * onehot, axis=1)
    position = flat * capacity + slot
    slot_count = n_tok * capacity
    hits = (position[:, None] == jnp.arange(slot_count, dtype=jnp.int32)[None, :]).astype(jnp.int32)
    hits = jnp.sum(hits.reshape(tok_dev, top_k, slot_count), axis=1)
    token_of = jnp.sum(hits * jnp.arange(tok_dev, dtype=jnp.int32)[:, None], axis=0)
    filled = jnp.sum(hits, axis=0) > 0
    return (position, token_of, filled)


def bucket(rows, token_of, filled):
    return jnp.where(filled[:, None], jnp.take(rows, token_of, axis=0), jnp.zeros((), rows.dtype))


def combine(returned, position, gate_vals):
    picked = jnp.take(returned, position, axis=0).reshape(
        gate_vals.shape[0], gate_vals.shape[1], returned.shape[1]
    )
    total = jnp.zeros((picked.shape[0], picked.shape[2]), jnp.float32)
    for column in range(gate_vals.shape[1]):
        total = total + gate_vals[:, column : column + 1] * picked[:, column].astype(jnp.float32)
    return total


def hidden_grads(gate_pre, up_pre, hidden_grad):
    sigma = jax.nn.sigmoid(gate_pre)
    silu_value = gate_pre * sigma
    slope = sigma * (1.0 + gate_pre * (1.0 - sigma))
    return (
        (hidden_grad * up_pre * slope).astype(jnp.bfloat16),
        (hidden_grad * silu_value).astype(jnp.bfloat16),
    )


def shards(activations, out_grad, routes, gate_vals, w_gate, w_up, w_down):
    n_tok = lax.axis_size("tok")
    tok_dev = routes.shape[0]
    top_k = routes.shape[1]
    capacity = max(2, 2 * tok_dev * top_k // n_tok)
    slot_count = n_tok * capacity
    gate_local = w_gate[0]
    up_local = w_up[0]
    down_local = w_down[0]
    contract_last = (((1,), (1,)), ((), ()))
    position, token_of, filled = routing(routes, n_tok, capacity)
    whole_x, whole_g = (
        lax.all_gather(activations, "tp", axis=1, tiled=True),
        lax.all_gather(out_grad, "tp", axis=1, tiled=True),
    )
    width = whole_x.shape[1]
    send_x = bucket(whole_x, token_of, filled).reshape(n_tok, capacity, width)
    send_g = bucket(whole_g, token_of, filled).reshape(n_tok, capacity, width)
    recv_x, recv_g = (
        lax.all_to_all(send_x, "tok", split_axis=0, concat_axis=0, tiled=True),
        lax.all_to_all(send_g, "tok", split_axis=0, concat_axis=0, tiled=True),
    )
    recv_x = recv_x.reshape(slot_count, width)
    recv_g = recv_g.reshape(slot_count, width)
    gate_pre = lax.dot_general(
        recv_x, gate_local, contract_last, preferred_element_type=jnp.float32
    )
    up_pre = lax.dot_general(recv_x, up_local, contract_last, preferred_element_type=jnp.float32)
    hidden_grad = lax.dot_general(
        recv_g, down_local, contract_last, preferred_element_type=jnp.float32
    )
    gate_grad, up_grad = hidden_grads(gate_pre, up_pre, hidden_grad)
    partial_value = jnp.dot(gate_grad, gate_local, preferred_element_type=jnp.float32)
    partial_value = partial_value + jnp.dot(up_grad, up_local, preferred_element_type=jnp.float32)
    partial_bf = partial_value.astype(jnp.bfloat16)
    full_width = partial_bf.shape[1]
    returned = lax.all_to_all(
        partial_bf.reshape(n_tok, capacity, full_width),
        "tok",
        split_axis=0,
        concat_axis=0,
        tiled=True,
    )
    combined = combine(returned.reshape(slot_count, full_width), position, gate_vals)
    summed = lax.psum_scatter(combined, "tp", scatter_dimension=1, tiled=True)
    return summed.astype(jnp.bfloat16)


def solution(mesh):
    placed = (
        P("tok", "tp"),
        P("tok", "tp"),
        P("tok", None),
        P("tok", None),
        P("tok", "tp", None),
        P("tok", "tp", None),
        P("tok", "tp", None),
    )
    return jax.shard_map(
        shards, mesh=mesh, in_specs=placed, out_specs=P("tok", "tp"), check_vma=False
    )
```

profile of v0, /device:TPU:16, one launch (start us, length us, event | category | flops | bytes accessed | tf_op | source)
XLA Modules:
  0.0 566.2 jit_solution(14401200045992333486)
XLA Ops:
  6.5 0.0 copy-start
  6.5 0.0 all-gather.3.cloned.1.call-start
  6.5 0.7 all-gather.3.cloned.1.call-update
  7.3 0.0 all-gather.5.cloned.1.call-start
  7.3 0.7 all-gather.5.cloned.1.call-update
  8.0 0.8 copy.23
  8.8 0.1 eq.40
  8.9 0.1 reshape.106
  9.1 0.6 reduce-window.6
  9.7 0.2 slice_reduce_fusion
  9.9 0.1 fusion.43
  10.0 0.1 reduce_sum.41
  10.2 0.1 copy.26
  10.3 0.7 compare_and_fusion.1
  11.0 0.1 convert_reduce_fusion.1
  11.2 31.5 %all-gather.3.cloned.1.call-done = bf16[128,4096]{1,0:T(8,128)(2,1)} async-done(((bf16[128,512]{1,0:T(8,128)(2,1)}), bf16[128,4096]{1,0:T(8,128)(2,1)}) %all-gather.3.cloned.1.call-update) | async-done | bytes 1048592 | tf_op jit(solution)/shard_map/all_gather | solution.py:60
  42.7 9.9 %gather_fusion.1 = bf16[512,4096]{1,0:T(8,128)(2,1)} fusion(bf16[128,4096]{1,0:T(8,128)(2,1)} %all-gather.3.cloned.1.call-done, s32[1024]{0:T(1024)S(1)} %pad_clamp_fusion.1), kind=kCustom, calls=%fused_computation.clone | custom fusion | bytes 8390656 | tf_op jit(solution)/shard_map/jit(_take)/gather | solution.py:24
  52.6 20.9 %all-gather.5.cloned.1.call-done = bf16[128,4096]{1,0:T(8,128)(2,1)} async-done(((bf16[128,512]{1,0:T(8,128)(2,1)}), bf16[128,4096]{1,0:T(8,128)(2,1)}) %all-gather.5.cloned.1.call-update) | async-done | bytes 1048592 | tf_op jit(solution)/shard_map/all_gather | solution.py:59
  73.5 9.9 %gather_fusion.2 = bf16[512,4096]{1,0:T(8,128)(2,1)} fusion(bf16[128,4096]{1,0:T(8,128)(2,1)} %all-gather.5.cloned.1.call-done, s32[1024]{0:T(1024)S(1)} %pad_clamp_fusion.1), kind=kCustom, calls=%fused_computation.1.clone | custom fusion | bytes 8390656 | tf_op jit(solution)/shard_map/jit(_take)/gather | solution.py:24
  83.4 5.4 fusion.7
  88.8 109.8 %all_to_all.15 = bf16[64,8,4096]{2,1,0:T(8,128)(2,1)} all-to-all(bf16[64,8,4096]{2,1,0:T(8,128)(2,1)S(1)} %get-tuple-element.12), channel_id=1, replica_groups=mesh['tok'=64,'tp'=8] {'tok'}, dimensions={0} | all-to-all | bytes 8388608 | tf_op jit(solution)/shard_map/all_to_all | solution.py:66
  198.5 0.0 copy-start.1
  198.5 16.3 %all-to-all-start = ((bf16[64,8,4096]{2,1,0:T(8,128)(2,1)}), bf16[64,8,4096]{2,1,0:T(8,128)(2,1)}, u32[]{:S(2)}, u32[]{:S(2)}) async-start(bf16[64,8,4096]{2,1,0:T(8,128)(2,1)} %get-tuple-element.13), calls=%async_computation | async-start | bytes 8388608 | tf_op jit(solution)/shard_map/all_to_all | solution.py:67
  214.9 0.0 copy-done.1
  214.9 3.7 fusion.1
  218.6 114.2 %all-to-all-done = bf16[64,8,4096]{2,1,0:T(8,128)(2,1)} async-done(((bf16[64,8,4096]{2,1,0:T(8,128)(2,1)}), bf16[64,8,4096]{2,1,0:T(8,128)(2,1)}, u32[]{:S(2)}, u32[]{:S(2)}) %all-to-all-start) | async-done | bytes 4194336 | tf_op jit(solution)/shard_map/all_to_all | solution.py:67
  332.8 5.0 fusion.5
  337.8 0.0 copy-done
  337.8 8.3 %fusion.10 = f32[512,4096]{1,0:T(8,128)} fusion(bf16[1,192,4096]{2,1,0:T(8,128)(2,1)S(1)} %copy-done.1, f32[512,192]{0,1:T(8,128)} %fusion.5, bf16[1,192,4096]{2,1,0:T(8,128)(2,1)S(1)} %copy-done, bf16[64,8,4096]{2,1,0:T(8,128)(2,1)} %all_to_all.15, f32[512,192]{0,1:T(8,128)S(1)} %fusion.1), kind=kOutput, calls=%fused_computation.19 | convolution fusion | flops 1611595776 | bytes 16515072 | tf_op jit(solution)/shard_map/dot_general | solution.py:79
  346.1 6.8 %fusion = bf16[64,8,4096]{2,1,0:T(8,128)(2,1)} fusion(f32[512,4096]{1,0:T(8,128)} %fusion.10, bf16[1,192,4096]{2,1,0:T(8,128)(2,1)S(1)} %copy-done, f32[512,192]{0,1:T(8,128)} %fusion.5, f32[512,192]{0,1:T(8,128)S(1)} %fusion.1), kind=kOutput, calls=%fused_computation.4 | convolution fusion | flops 810090496 | bytes 14942208 | tf_op jit(solution)/shard_map/dot_general | solution.py:80
  353.0 0.0 copy-start.2
  353.0 0.0 copy-start.3
  353.0 15.8 %all-to-all-start.2 = ((bf16[64,8,4096]{2,1,0:T(8,128)(2,1)}), bf16[64,8,4096]{2,1,0:T(8,128)(2,1)}, u32[]{:S(2)}, u32[]{:S(2)}) async-start(bf16[64,8,4096]{2,1,0:T(8,128)(2,1)} %fusion), calls=%async_computation.2 | async-start | bytes 8388608 | tf_op jit(solution)/shard_map/all_to_all | solution.py:83
  368.8 0.3 reduce-scatter.2.cloned.1.call-start
  369.1 0.0 copy-done.2
  369.1 0.1 copy.27
  369.2 0.1 mul.84
  369.4 0.0 copy-done.3
  369.4 110.9 %all-to-all-done.2 = bf16[64,8,4096]{2,1,0:T(8,128)(2,1)} async-done(((bf16[64,8,4096]{2,1,0:T(8,128)(2,1)}), bf16[64,8,4096]{2,1,0:T(8,128)(2,1)}, u32[]{:S(2)}, u32[]{:S(2)}) %all-to-all-start.2) | async-done | bytes 4194336 | tf_op jit(solution)/shard_map/all_to_all | solution.py:83
  480.3 7.9 %gather_fusion = bf16[256,4096]{1,0:T(8,128)(2,1)} fusion(bf16[512,4096]{1,0:T(8,128)(2,1)} %bitcast.10, s32[1024]{0:T(1024)S(1)} %pad_clamp_fusion), kind=kCustom, calls=%fused_computation.2 | custom fusion | bytes 4195328 | tf_op jit(solution)/shard_map/jit(_take)/gather | solution.py:28
  488.3 4.4 gather.10
  492.7 4.0 copy_select_fusion
  496.7 1.8 fusion.9
  498.5 0.0 reduce-scatter.2.cloned.1.call-update
  498.5 59.6 %reduce-scatter.2.cloned.1.call-done = f32[128,512]{1,0:T(8,128)} async-done(((f32[128,4096]{1,0:T(8,128)}), f32[128,512]{1,0:T(8,128)}) %reduce-scatter.2.cloned.1.call-update) | async-done | bytes 262160 | tf_op jit(solution)/shard_map/reduce_scatter | solution.py:91
  558.1 1.6 convert_element_type.45
  (11 shorter events, 0.1 us)
Async XLA Ops:
  6.5 331.3 %copy-start = (bf16[1,192,4096]{2,1,0:T(8,128)(2,1)S(1)}, bf16[1,192,4096]{2,1,0:T(8,128)(2,1)}, u32[]{:S(2)}) copy-start(bf16[1,192,4096]{2,1,0:T(8,128)(2,1)} %param.14) | copy-start | bytes 4718596
  6.5 36.1 %all-gather.3.cloned.1.call-start = ((), (), s32[]{:S(2)}) async-start(), calls=%async_computation.4 | async-start | bytes 1179648 | tf_op jit(solution)/shard_map/all_gather | solution.py:60
  7.3 66.2 %all-gather.5.cloned.1.call-start = ((), (), s32[]{:S(2)}) async-start(), calls=%async_computation.5 | async-start | bytes 1179648 | tf_op jit(solution)/shard_map/all_gather | solution.py:59
  198.5 16.4 %copy-start.1 = (bf16[1,192,4096]{2,1,0:T(8,128)(2,1)S(1)}, bf16[1,192,4096]{2,1,0:T(8,128)(2,1)}, u32[]{:S(2)}) copy-start(bf16[1,192,4096]{2,1,0:T(8,128)(2,1)} %param.13) | copy-start | bytes 4718596
  198.5 134.3 %all-to-all-start = ((bf16[64,8,4096]{2,1,0:T(8,128)(2,1)}), bf16[64,8,4096]{2,1,0:T(8,128)(2,1)}, u32[]{:S(2)}, u32[]{:S(2)}) async-start(bf16[64,8,4096]{2,1,0:T(8,128)(2,1)} %get-tuple-element.13), calls=%async_computation | async-start | bytes 8388608 | tf_op jit(solution)/shard_map/all_to_all | solution.py:67
  353.0 16.1 %copy-start.2 = (s32[128,2]{0,1:T(2,128)S(1)}, s32[128,2]{0,1:T(2,128)}, u32[]{:S(2)}) copy-start(s32[128,2]{0,1:T(2,128)} %param.11) | copy-start | bytes 3076
  353.0 16.4 %copy-start.3 = (f32[128,2]{0,1:T(2,128)S(1)}, f32[128,2]{0,1:T(2,128)}, u32[]{:S(2)}) copy-start(f32[128,2]{0,1:T(2,128)} %param.12) | copy-start | bytes 3076
  353.0 127.4 %all-to-all-start.2 = ((bf16[64,8,4096]{2,1,0:T(8,128)(2,1)}), bf16[64,8,4096]{2,1,0:T(8,128)(2,1)}, u32[]{:S(2)}, u32[]{:S(2)}) async-start(bf16[64,8,4096]{2,1,0:T(8,128)(2,1)} %fusion), calls=%async_computation.2 | async-start | bytes 8388608 | tf_op jit(solution)/shard_map/all_to_all | solution.py:83
  368.8 189.3 %reduce-scatter.2.cloned.1.call-start = ((), (), s32[]{:S(2)}) async-start(), calls=%async_computation.6 | async-start | bytes 2359296 | tf_op jit(solution)/shard_map/reduce_scatter | solution.py:91
Sparse Core Ops, SparseCore 0:
  9.5 33.1 all-gather.2
  44.8 28.5 all-gather.4
  498.6 59.3 reduce-scatter.1
where the time goes:
time: 567 us; the launch traced here: 566 us
  waiting for transfers between devices  338 us (60%)
  blocking collectives  110 us (19%)
  local copies, waits for them, and re-layouts  33.9 us (6%)
  starting transfers between devices  32.5 us (6%)
  matrix products  23.8 us (4%)
  other arithmetic  14.5 us (3%)
  between operations  13.2 us (2%)
    all_to_all x1, waiting for transfers between devices, shards(): lax.all_to_all(send_g, 'tok', split_axis=0, concat_axis=0, tiled=True)  114 us
    all_to_all x1, waiting for transfers between devices, shards(): lax.all_to_all(partial_bf.reshape(n_tok, capacity, full_width), 'tok', sp...  111 us
    all_to_all x1, blocking collectives, shards(): lax.all_to_all(send_x, 'tok', split_axis=0, concat_axis=0, tiled=True)  110 us
    reduce_scatter x1, waiting for transfers between devices, shards(): summed = lax.psum_scatter(combined, 'tp', scatter_dimension=1, tiled=True)  59.6 us
    all_gather x1, waiting for transfers between devices, shards(): lax.all_gather(out_grad, 'tp', axis=1, tiled=True)  31.5 us
    all_gather x1, waiting for transfers between devices, shards(): lax.all_gather(activations, 'tp', axis=1, tiled=True)  20.9 us
    gather x2, local copies, waits for them, and re-layouts, bucket(): jnp.take(rows, token_of, axis=0)  19.8 us
    all_to_all x1, starting transfers between devices, shards(): lax.all_to_all(send_g, 'tok', split_axis=0, concat_axis=0, tiled=True)  16.3 us
  transfers between devices with their start and end apart: 5, of which 5 were waited for; matrix products, arithmetic and copies ran while one was open for 3% of the time, Pallas kernels for 0%

commit v1 on v0

--- a/solution.py
+++ b/solution.py
@@ -2,6 +2,13 @@
 import jax.numpy as jnp
 from jax import lax
 from jax.sharding import PartitionSpec as P
+
+
+def gather_over(array, name, dim):
+    size = lax.axis_size(name)
+    blocks = jnp.stack([array for _ in range(size)])
+    blocks = lax.all_to_all(blocks, name, split_axis=0, concat_axis=0)
+    return jnp.concatenate(blocks, axis=dim)
 
 
 def routing(routes, n_tok, capacity):
@@ -56,7 +63,7 @@
     contract_last = (((1,), (1,)), ((), ()))
     position, token_of, filled = routing(routes, n_tok, capacity)
     whole_x, whole_g = (
-        lax.all_gather(activations, "tp", axis=1, tiled=True),
+        gather_over(activations, "tp", 1),
         lax.all_gather(out_grad, "tp", axis=1, tiled=True),
     )
     width = whole_x.shape[1]

time: 567 us -> 536 us (0.945)
  the two profiles are of different devices: /device:TPU:16 before, /device:TPU:8 now
where the time goes in v1:
time: 536 us; the launch traced here: 535 us
  waiting for transfers between devices  305 us (57%)
  blocking collectives  111 us (21%)
  starting transfers between devices  36 us (7%)
  local copies, waits for them, and re-layouts  32.1 us (6%)
  matrix products  23.8 us (4%)
  other arithmetic  13.8 us (3%)
  between operations  13.5 us (3%)
    all_to_all x1, waiting for transfers between devices, shards(): lax.all_to_all(send_g, 'tok', split_axis=0, concat_axis=0, tiled=True)  114 us
    all_to_all x1, waiting for transfers between devices, shards(): lax.all_to_all(partial_bf.reshape(n_tok, capacity, full_width), 'tok', sp...  113 us
    all_to_all x1, blocking collectives, shards(): lax.all_to_all(send_x, 'tok', split_axis=0, concat_axis=0, tiled=True)  111 us
    reduce_scatter x1, waiting for transfers between devices, shards(): summed = lax.psum_scatter(combined, 'tp', scatter_dimension=1, tiled=True)  56.7 us
    all_to_all x1, starting transfers between devices, shards(): lax.all_to_all(partial_bf.reshape(n_tok, capacity, full_width), 'tok', sp...  16.1 us
    all_to_all x1, starting transfers between devices, shards(): lax.all_to_all(send_g, 'tok', split_axis=0, concat_axis=0, tiled=True)  15.3 us
    gather x2, local copies, waits for them, and re-layouts, bucket(): jnp.take(rows, token_of, axis=0)  14.3 us
    all_to_all x1, waiting for transfers between devices, gather_over(): blocks = lax.all_to_all(blocks, name, split_axis=0, concat_axis=0)  14.1 us
  transfers between devices with their start and end apart: 5, of which 5 were waited for; matrix products, arithmetic and copies ran while one was open for 3% of the time, Pallas kernels for 0%

profile of v1, /device:TPU:8, one launch (start us, length us, event | category | flops | bytes accessed | tf_op | source)
XLA Modules:
  0.0 535.4 jit_solution(11491883764416016530)
XLA Ops:
  6.5 0.0 copy-start
  6.5 0.0 copy-start.3
  6.5 0.0 all-gather.2.cloned.1.call-start
  6.5 0.7 all-gather.2.cloned.1.call-update
  7.3 2.0 stack.2
  9.3 4.3 all-to-all-start.1
  13.6 0.0 copy-done.3
  13.6 0.1 copy.31
  13.7 0.1 eq.40
  13.8 0.1 reshape.114
  14.0 0.6 reduce-window.6
  14.6 0.2 slice_reduce_fusion
  14.8 0.1 fusion.43
  15.0 0.1 reduce_sum.41
  15.1 0.1 copy.34
  15.2 0.1 convert_reduce_fusion.1
  15.4 14.1 %all-to-all-done.1 = bf16[8,128,512]{2,1,0:T(8,128)(2,1)S(1)} async-done(((bf16[8,128,512]{2,1,0:T(8,128)(2,1)}), bf16[8,128,512]{2,1,0:T(8,128)(2,1)S(1)}, u32[]{:S(2)}, u32[]{:S(2)}) %all-to-all-start.1) | async-done | bytes 1048608 | tf_op jit(solution)/shard_map/all_to_all | solution.py:10
  29.6 0.0 copy-start.1
  29.6 1.0 copy-done.1
  30.6 1.3 copy.39
  31.9 4.4 gather_fusion.2
  36.3 6.4 %all-gather.2.cloned.1.call-done = bf16[128,4096]{1,0:T(8,128)(2,1)} async-done(((bf16[128,512]{1,0:T(8,128)(2,1)}), bf16[128,4096]{1,0:T(8,128)(2,1)}) %all-gather.2.cloned.1.call-update) | async-done | bytes 1048592 | tf_op jit(solution)/shard_map/all_gather | solution.py:67
  42.8 9.9 %gather_fusion.1 = bf16[512,4096]{1,0:T(8,128)(2,1)} fusion(bf16[128,4096]{1,0:T(8,128)(2,1)} %all-gather.2.cloned.1.call-done, s32[1024]{0:T(1024)S(1)} %pad_clamp_fusion.1), kind=kCustom, calls=%fused_computation.clone | custom fusion | bytes 8390656 | tf_op jit(solution)/shard_map/jit(_take)/gather | solution.py:31
  52.7 5.3 fusion.7
  58.0 110.9 %all_to_all.20 = bf16[64,8,4096]{2,1,0:T(8,128)(2,1)} all-to-all(bf16[64,8,4096]{2,1,0:T(8,128)(2,1)S(1)} %get-tuple-element.12), channel_id=1, replica_groups=mesh['tok'=64,'tp'=8] {'tok'}, dimensions={0} | all-to-all | bytes 8388608 | tf_op jit(solution)/shard_map/all_to_all | solution.py:73
  168.9 0.0 copy-start.2
  168.9 15.3 %all-to-all-start = ((bf16[64,8,4096]{2,1,0:T(8,128)(2,1)}), bf16[64,8,4096]{2,1,0:T(8,128)(2,1)}, u32[]{:S(2)}, u32[]{:S(2)}) async-start(bf16[64,8,4096]{2,1,0:T(8,128)(2,1)} %get-tuple-element.13), calls=%async_computation | async-start | bytes 8388608 | tf_op jit(solution)/shard_map/all_to_all | solution.py:74
  184.2 0.0 copy-done.2
  184.2 3.7 fusion.1
  187.9 114.0 %all-to-all-done = bf16[64,8,4096]{2,1,0:T(8,128)(2,1)} async-done(((bf16[64,8,4096]{2,1,0:T(8,128)(2,1)}), bf16[64,8,4096]{2,1,0:T(8,128)(2,1)}, u32[]{:S(2)}, u32[]{:S(2)}) %all-to-all-start) | async-done | bytes 4194336 | tf_op jit(solution)/shard_map/all_to_all | solution.py:74
  301.9 5.0 fusion.5
  306.9 0.0 copy-done
  306.9 8.3 %fusion.10 = f32[512,4096]{1,0:T(8,128)} fusion(bf16[1,192,4096]{2,1,0:T(8,128)(2,1)S(1)} %copy-done.2, f32[512,192]{0,1:T(8,128)} %fusion.5, bf16[1,192,4096]{2,1,0:T(8,128)(2,1)S(1)} %copy-done, bf16[64,8,4096]{2,1,0:T(8,128)(2,1)} %all_to_all.20, f32[512,192]{0,1:T(8,128)S(1)} %fusion.1), kind=kOutput, calls=%fused_computation.19 | convolution fusion | flops 1611595776 | bytes 16515072 | tf_op jit(solution)/shard_map/dot_general | solution.py:86
  315.2 6.8 %fusion = bf16[64,8,4096]{2,1,0:T(8,128)(2,1)} fusion(f32[512,4096]{1,0:T(8,128)} %fusion.10, bf16[1,192,4096]{2,1,0:T(8,128)(2,1)S(1)} %copy-done, f32[512,192]{0,1:T(8,128)} %fusion.5, f32[512,192]{0,1:T(8,128)S(1)} %fusion.1), kind=kOutput, calls=%fused_computation.4 | convolution fusion | flops 810090496 | bytes 14942208 | tf_op jit(solution)/shard_map/dot_general | solution.py:87
  322.0 0.0 copy-start.4
  322.0 16.1 %all-to-all-start.3 = ((bf16[64,8,4096]{2,1,0:T(8,128)(2,1)}), bf16[64,8,4096]{2,1,0:T(8,128)(2,1)}, u32[]{:S(2)}, u32[]{:S(2)}) async-start(bf16[64,8,4096]{2,1,0:T(8,128)(2,1)} %fusion), calls=%async_computation.3 | async-start | bytes 8388608 | tf_op jit(solution)/shard_map/all_to_all | solution.py:90
  338.1 0.3 reduce-scatter.2.cloned.1.call-start
  338.4 0.1 copy.36
  338.5 0.1 mul.84
  338.7 0.0 copy-done.4
  338.7 113.3 %all-to-all-done.3 = bf16[64,8,4096]{2,1,0:T(8,128)(2,1)} async-done(((bf16[64,8,4096]{2,1,0:T(8,128)(2,1)}), bf16[64,8,4096]{2,1,0:T(8,128)(2,1)}, u32[]{:S(2)}, u32[]{:S(2)}) %all-to-all-start.3) | async-done | bytes 4194336 | tf_op jit(solution)/shard_map/all_to_all | solution.py:90
  452.0 7.9 %gather_fusion = bf16[256,4096]{1,0:T(8,128)(2,1)} fusion(bf16[512,4096]{1,0:T(8,128)(2,1)} %bitcast.11, s32[1024]{0:T(1024)S(1)} %pad_clamp_fusion), kind=kCustom, calls=%fused_computation.2 | custom fusion | bytes 4195328 | tf_op jit(solution)/shard_map/jit(_take)/gather | solution.py:35
  460.0 4.4 gather.10
  464.4 4.0 copy_select_fusion
  468.4 1.8 fusion.9
  470.2 0.0 reduce-scatter.2.cloned.1.call-update
  470.2 56.7 %reduce-scatter.2.cloned.1.call-done = f32[128,512]{1,0:T(8,128)} async-done(((f32[128,4096]{1,0:T(8,128)}), f32[128,512]{1,0:T(8,128)}) %reduce-scatter.2.cloned.1.call-update) | async-done | bytes 262160 | tf_op jit(solution)/shard_map/reduce_scatter | solution.py:98
  526.9 1.6 convert_element_type.45
  (12 shorter events, 0.2 us)
Async XLA Ops:
  6.5 300.3 %copy-start = (bf16[1,192,4096]{2,1,0:T(8,128)(2,1)S(1)}, bf16[1,192,4096]{2,1,0:T(8,128)(2,1)}, u32[]{:S(2)}) copy-start(bf16[1,192,4096]{2,1,0:T(8,128)(2,1)} %param.14) | copy-start | bytes 4718596
  6.5 7.1 %copy-start.3 = (s32[128,2]{0,1:T(2,128)S(1)}, s32[128,2]{0,1:T(2,128)}, u32[]{:S(2)}) copy-start(s32[128,2]{0,1:T(2,128)} %param.11) | copy-start | bytes 3076
  6.5 36.2 %all-gather.2.cloned.1.call-start = ((), (), s32[]{:S(2)}) async-start(), calls=%async_computation.5 | async-start | bytes 1179648 | tf_op jit(solution)/shard_map/all_gather | solution.py:67
  9.3 20.3 %all-to-all-start.1 = ((bf16[8,128,512]{2,1,0:T(8,128)(2,1)}), bf16[8,128,512]{2,1,0:T(8,128)(2,1)S(1)}, u32[]{:S(2)}, u32[]{:S(2)}) async-start(bf16[8,128,512]{2,1,0:T(8,128)(2,1)} %stack.2), calls=%async_computation.1 | async-start | bytes 2097152 | tf_op jit(solution)/shard_map/all_to_all | solution.py:10
  29.6 1.0 copy-start.1
  168.9 15.3 %copy-start.2 = (bf16[1,192,4096]{2,1,0:T(8,128)(2,1)S(1)}, bf16[1,192,4096]{2,1,0:T(8,128)(2,1)}, u32[]{:S(2)}) copy-start(bf16[1,192,4096]{2,1,0:T(8,128)(2,1)} %param.13) | copy-start | bytes 4718596
  168.9 133.0 %all-to-all-start = ((bf16[64,8,4096]{2,1,0:T(8,128)(2,1)}), bf16[64,8,4096]{2,1,0:T(8,128)(2,1)}, u32[]{:S(2)}, u32[]{:S(2)}) async-start(bf16[64,8,4096]{2,1,0:T(8,128)(2,1)} %get-tuple-element.13), calls=%async_computation | async-start | bytes 8388608 | tf_op jit(solution)/shard_map/all_to_all | solution.py:74
  322.0 16.7 %copy-start.4 = (f32[128,2]{0,1:T(2,128)S(1)}, f32[128,2]{0,1:T(2,128)}, u32[]{:S(2)}) copy-start(f32[128,2]{0,1:T(2,128)} %param.12) | copy-start | bytes 3076
  322.0 130.0 %all-to-all-start.3 = ((bf16[64,8,4096]{2,1,0:T(8,128)(2,1)}), bf16[64,8,4096]{2,1,0:T(8,128)(2,1)}, u32[]{:S(2)}, u32[]{:S(2)}) async-start(bf16[64,8,4096]{2,1,0:T(8,128)(2,1)} %fusion), calls=%async_computation.3 | async-start | bytes 8388608 | tf_op jit(solution)/shard_map/all_to_all | solution.py:90
  338.1 188.8 %reduce-scatter.2.cloned.1.call-start = ((), (), s32[]{:S(2)}) async-start(), calls=%async_computation.6 | async-start | bytes 2359296 | tf_op jit(solution)/shard_map/reduce_scatter | solution.py:98
Sparse Core Ops, SparseCore 0:
  9.5 33.2 all-gather.1
  470.3 56.5 reduce-scatter.1
